TPU v7x, 32 devices: a whole 2x2x4 slice. The times are simulated.
32 devices in a mesh: dp: 8 (over y, x, core), shard: 4 (over z).
Axes of the slice: x: 2, y: 2, z: 4, core: 2. Of those that a mesh axis runs over, the one named last changes fastest.
Arguments:
- tokens: bfloat16 [16384, 1024], P(('dp', 'shard')), may hold values from -9 to 9
- lengths: int32 [32, 2], P(('dp', 'shard')), may hold values from 8 to 256, as said below
- w_qkv: bfloat16 [2, 1024, 3072], P(None, ('dp', 'shard')), may hold values from -0.1875 to 0.1875
- w_out: bfloat16 [2, 1024, 1024], P(None, ('dp', 'shard')), may hold values from -2 to 2
- w_up: bfloat16 [2, 1024, 4096], P(None, ('dp', 'shard')), may hold values from -0.1875 to 0.1875
- w_down: bfloat16 [2, 4096, 1024], P(None, ('dp', 'shard')), may hold values from -0.09375 to 0.09375
- ln_gain: float32 [2, 2, 1024], replicated, may hold values from 0.5 to 1.5
- bias_qv: float32 [2, 2, 1024], replicated, may hold values from -3 to 3
- bias_out: float32 [2, 1024], replicated, may hold values from -3 to 3
- ln_bias: float32 [2, 2, 1024], replicated, may hold values from -3 to 3
- bias_up: float32 [2, 4096], replicated, may hold values from -3 to 3
- bias_down: float32 [2, 1024], replicated, may hold values from -3 to 3
- cotangent: bfloat16 [16384, 1024], P(('dp', 'shard')), may hold values from -6 to 6
Outputs:
- activations: bfloat16 [16384, 1024], P(('dp', 'shard'))
- input_grad: float32 [16384, 1024], P(('dp', 'shard'))
- grad_bias_qv: float32 [2, 2, 1024], replicated
- grad_bias_out: float32 [2, 1024], replicated
- grad_ln_bias: float32 [2, 2, 1024], replicated
- grad_bias_up: float32 [2, 4096], replicated
- grad_bias_down: float32 [2, 1024], replicated
- rms_values: float32 [2, 3], replicated
Inputs may be any that keep to these rules, and one draw needn't show every extreme that they name: `lengths`: each packed row holds two sentences from its first slot on, one of exactly 256 tokens; the remaining slots are padding.
All inputs are finite; a program needn't handle non-finite values.
Results may differ from a plain program's by a relative error of at most 0.022.
Values may be sent and summed in bfloat16 or wider, within the bound.
A program may use at most 256 MiB of HBM per device.

v0:
```python
import jax
import jax.numpy as jnp
from jax import lax
from jax.sharding import PartitionSpec as P

HEADS = 16


norm_eps = 1e-06


def mat_dot(left_side, right_side):
    return jnp.dot(left_side, right_side, preferred_element_type=jnp.float32)


def back_dot(left_side, right_side):
    return lax.dot_general(
        left_side, right_side, (((1,), (1,)), ((), ())), preferred_element_type=jnp.float32
    )


def normalize(stream, gain_row, shift_row):
    mean_row = jnp.mean(stream, axis=-1, keepdims=True)
    centred = stream - mean_row
    variance = jnp.mean(centred * centred, axis=-1, keepdims=True)
    inv_std = lax.rsqrt(variance + norm_eps)
    normed = centred * inv_std
    return (normed * gain_row + shift_row, normed, inv_std)


def norm_back(grad_out, gain_row, normed, inv_std):
    scaled = grad_out * gain_row
    return inv_std * (
        scaled
        - jnp.mean(scaled, axis=-1, keepdims=True)
        - normed * jnp.mean(scaled * normed, axis=-1, keepdims=True)
    )


def gelu_slope(pre_act):
    cumulative = 0.5 * (1.0 + lax.erf(pre_act * 0.7071067811865476))
    density = jnp.exp(-0.5 * pre_act * pre_act) * 0.3989422804014327
    return cumulative + pre_act * density


def segments(lengths, slot_count):
    first_end = lengths[0, 0]
    second_end = first_end + lengths[0, 1]
    position = jnp.arange(slot_count, dtype=jnp.int32)
    segment = (position >= first_end).astype(jnp.int32) + (position >= second_end).astype(jnp.int32)
    return (segment, position < second_end)


def split_heads(matrix):
    return matrix.reshape(matrix.shape[0], HEADS, matrix.shape[1] // HEADS)


def masked_scores(queries, keys_part, same_seg):
    score_scale = (queries.shape[1] // HEADS) ** (-0.5)
    scores = (
        jnp.einsum(
            "qhd,khd->hqk",
            split_heads(queries),
            split_heads(keys_part),
            preferred_element_type=jnp.float32,
        )
        * score_scale
    )
    return jnp.where(same_seg[None], scores, -1e30)


def attend(queries, keys_part, values_part, same_seg):
    scores = masked_scores(queries, keys_part, same_seg)
    row_max = jnp.max(scores, axis=-1, keepdims=True)
    exponent = jnp.exp(scores - row_max)
    row_total = jnp.sum(exponent, axis=-1, keepdims=True)
    probs = exponent / row_total
    log_total = row_max + jnp.log(row_total)
    mixed = jnp.einsum(
        "hqk,khd->qhd",
        probs.astype(jnp.bfloat16),
        split_heads(values_part),
        preferred_element_type=jnp.float32,
    )
    return (mixed.reshape(queries.shape).astype(jnp.bfloat16), log_total)


def attend_back(queries, keys_part, values_part, log_total, same_seg, grad_mixed):
    score_scale = (queries.shape[1] // HEADS) ** (-0.5)
    probs = jnp.exp(masked_scores(queries, keys_part, same_seg) - log_total)
    grad_heads = split_heads(grad_mixed)
    grad_probs = jnp.einsum(
        "qhd,khd->hqk", grad_heads, split_heads(values_part), preferred_element_type=jnp.float32
    )
    grad_values = jnp.einsum(
        "hqk,qhd->khd", probs.astype(jnp.bfloat16), grad_heads, preferred_element_type=jnp.float32
    )
    inner_sum = jnp.sum(probs * grad_probs, axis=-1, keepdims=True)
    grad_scores = (probs * (grad_probs - inner_sum)).astype(jnp.bfloat16)
    grad_queries = (
        jnp.einsum(
            "hqk,khd->qhd", grad_scores, split_heads(keys_part), preferred_element_type=jnp.float32
        )
        * score_scale
    )
    grad_keys = (
        jnp.einsum(
            "hqk,qhd->khd", grad_scores, split_heads(queries), preferred_element_type=jnp.float32
        )
        * score_scale
    )
    shape_out = queries.shape
    return (
        grad_queries.reshape(shape_out),
        grad_keys.reshape(shape_out),
        grad_values.reshape(shape_out),
    )


def local(
    tokens,
    lengths,
    w_qkv,
    w_out,
    w_up,
    w_down,
    ln_gain,
    bias_qv,
    bias_out,
    ln_bias,
    bias_up,
    bias_down,
    cotangent,
):
    slot_count, model_width = tokens.shape
    layer_count = w_qkv.shape[0]
    segment, valid_mask = segments(lengths, slot_count)
    same_seg = segment[:, None] == segment[None, :]
    valid_col = valid_mask.astype(jnp.float32)[:, None]
    stream = tokens.astype(jnp.float32)
    stored = []
    square_list = []
    for layer_at in range(layer_count):
        mat_qkv, mat_out, mat_up, mat_down = (
            lax.all_gather(w_qkv[layer_at], ("dp", "shard"), axis=0, tiled=True),
            lax.all_gather(w_out[layer_at], ("dp", "shard"), axis=0, tiled=True),
            lax.all_gather(w_up[layer_at], ("dp", "shard"), axis=0, tiled=True),
            lax.all_gather(w_down[layer_at], ("dp", "shard"), axis=0, tiled=True),
        )
        projected = mat_dot(stream.astype(jnp.bfloat16), mat_qkv)
        queries = (projected[:, 0:model_width] + bias_qv[layer_at, 0]).astype(jnp.bfloat16)
        keys_part = projected[:, model_width : 2 * model_width].astype(jnp.bfloat16)
        values_part = (projected[:, 2 * model_width :] + bias_qv[layer_at, 1]).astype(jnp.bfloat16)
        mixed, log_total = attend(queries, keys_part, values_part, same_seg)
        branch = mat_dot(mixed, mat_out) + bias_out[layer_at]
        first_out, normed_first, inv_first = normalize(
            stream + branch, ln_gain[layer_at, 0], ln_bias[layer_at, 0]
        )
        pre_act = mat_dot(first_out.astype(jnp.bfloat16), mat_up) + bias_up[layer_at]
        activated = jax.nn.gelu(pre_act, approximate=False).astype(jnp.bfloat16)
        ffn_out = mat_dot(activated, mat_down) + bias_down[layer_at]
        next_stream, normed_second, inv_second = normalize(
            first_out + ffn_out, ln_gain[layer_at, 1], ln_bias[layer_at, 1]
        )
        square_list.append(
            jnp.stack(
                [
                    jnp.sum(valid_col * stream * stream),
                    jnp.sum(valid_col * branch * branch),
                    jnp.sum(valid_col * ffn_out * ffn_out),
                ]
            )
        )
        stored.append(
            (
                queries,
                keys_part,
                values_part,
                log_total,
                normed_first,
                inv_first,
                pre_act,
                normed_second,
                inv_second,
            )
        )
        stream = next_stream
    activations = stream.astype(jnp.bfloat16)
    square_sums = jnp.stack(square_list)
    valid_count = jnp.sum(lengths).astype(jnp.float32)
    square_sums, valid_count = lax.psum((square_sums, valid_count), ("dp", "shard"))
    grad_stream = cotangent.astype(jnp.float32) * valid_col
    grad_layers = [None] * layer_count
    for layer_at in reversed(range(layer_count)):
        (
            queries,
            keys_part,
            values_part,
            log_total,
            normed_first,
            inv_first,
            pre_act,
            normed_second,
            inv_second,
        ) = stored[layer_at]
        mat_qkv, mat_out, mat_up, mat_down = (
            lax.all_gather(w_qkv[layer_at], ("dp", "shard"), axis=0, tiled=True),
            lax.all_gather(w_out[layer_at], ("dp", "shard"), axis=0, tiled=True),
            lax.all_gather(w_up[layer_at], ("dp", "shard"), axis=0, tiled=True),
            lax.all_gather(w_down[layer_at], ("dp", "shard"), axis=0, tiled=True),
        )
        grad_ln_second = jnp.sum(grad_stream, axis=0)
        grad_second = norm_back(grad_stream, ln_gain[layer_at, 1], normed_second, inv_second)
        grad_down_bias = jnp.sum(grad_second, axis=0)
        grad_pre = back_dot(grad_second.astype(jnp.bfloat16), mat_down) * gelu_slope(pre_act)
        grad_up_bias = jnp.sum(grad_pre, axis=0)
        grad_first = grad_second + back_dot(grad_pre.astype(jnp.bfloat16), mat_up)
        grad_ln_first = jnp.sum(grad_first, axis=0)
        grad_inner = norm_back(grad_first, ln_gain[layer_at, 0], normed_first, inv_first)
        grad_out_bias = jnp.sum(grad_inner, axis=0)
        grad_mixed = back_dot(grad_inner.astype(jnp.bfloat16), mat_out).astype(jnp.bfloat16)
        grad_queries, grad_keys, grad_values = attend_back(
            queries, keys_part, values_part, log_total, same_seg, grad_mixed
        )
        grad_qv_bias = jnp.stack([jnp.sum(grad_queries, axis=0), jnp.sum(grad_values, axis=0)])
        grad_proj = jnp.concatenate([grad_queries, grad_keys, grad_values], axis=1).astype(
            jnp.bfloat16
        )
        grad_stream = grad_inner + back_dot(grad_proj, mat_qkv)
        layer_terms = (
            grad_qv_bias,
            grad_out_bias,
            jnp.stack([grad_ln_first, grad_ln_second]),
            grad_up_bias,
            grad_down_bias,
        )
        layer_terms = lax.psum(
            (layer_terms[0], layer_terms[1], layer_terms[2], layer_terms[3], layer_terms[4]),
            ("dp", "shard"),
        )
        grad_layers[layer_at] = layer_terms
    grad_qv_all = jnp.stack([terms[0] for terms in grad_layers])
    grad_out_all = jnp.stack([terms[1] for terms in grad_layers])
    grad_ln_all = jnp.stack([terms[2] for terms in grad_layers])
    grad_up_all = jnp.stack([terms[3] for terms in grad_layers])
    grad_down_all = jnp.stack([terms[4] for terms in grad_layers])
    rms_values = jnp.sqrt(square_sums / (valid_count * model_width))
    return (
        activations,
        grad_stream,
        grad_qv_all,
        grad_out_all,
        grad_ln_all,
        grad_up_all,
        grad_down_all,
        rms_values,
    )


def solution(mesh):
    in_specs = (
        P(("dp", "shard"), None),
        P(("dp", "shard"), None),
        P(None, ("dp", "shard"), None),
        P(None, ("dp", "shard"), None),
        P(None, ("dp", "shard"), None),
        P(None, ("dp", "shard"), None),
        P(),
        P(),
        P(),
        P(),
        P(),
        P(),
        P(("dp", "shard"), None),
    )
    out_specs = (P(("dp", "shard"), None), P(("dp", "shard"), None), P(), P(), P(), P(), P(), P())
    return jax.shard_map(local, mesh=mesh, in_specs=in_specs, out_specs=out_specs, check_vma=False)
```

profile of v0, /device:TPU:0, one launch (start us, length us, event | category | flops | bytes accessed | tf_op | source)
XLA Modules:
  0.0 838.3 jit_solution(15583604867643429088)
XLA Ops:
  31.6 51.8 %all-gather.17.cloned.1.call-done = bf16[1,1024,3072]{2,1,0:T(8,128)(2,1)} async-done(((bf16[1,32,3072]{2,1,0:T(8,128)(2,1)}), bf16[1,1024,3072]{2,1,0:T(8,128)(2,1)}) %all-gather.17.cloned.1.call-update) | async-done | bytes 6291472 | tf_op jit(solution)/shard_map/all_gather | solution.py:145
  118.8 23.0 %all-gather.19.cloned.1.call-done = bf16[1,1024,1024]{2,1,0:T(8,128)(2,1)} async-done(((bf16[1,32,1024]{2,1,0:T(8,128)(2,1)}), bf16[1,1024,1024]{2,1,0:T(8,128)(2,1)}) %all-gather.19.cloned.1.call-update) | async-done | bytes 2097168 | tf_op jit(solution)/shard_map/all_gather | solution.py:146
  147.0 73.7 %all-gather.21.cloned.1.call-done = bf16[1,1024,4096]{2,1,0:T(8,128)(2,1)} async-done(((bf16[1,32,4096]{2,1,0:T(8,128)(2,1)}), bf16[1,1024,4096]{2,1,0:T(8,128)(2,1)}) %all-gather.21.cloned.1.call-update) | async-done | bytes 8388624 | tf_op jit(solution)/shard_map/all_gather | solution.py:147
  220.8 10.3 %fusion.38 = f32[512,4096]{1,0:T(8,128)} fusion(bf16[1,1024,4096]{2,1,0:T(8,128)(2,1)} %all-gather.21.cloned.1.call-done, f32[512,1024]{1,0:T(8,128)S(1)} %get-tuple-element.57, f32[1024]{0:T(1024)S(1)} %bitcast.255, f32[1024]{0:T(1024)S(1)} %bitcast.212, f32[512]{0:T(512)S(1)} %add_rsqrt_fusion.3, f32[512]{0:T(512)S(1)} %broadcast_multiply_fusion.11), kind=kOutput, calls=%fused_computation.52 | convolution fusion | flops 4297588736 | bytes 18886656 | tf_op jit(solution)/shard_map/dot_general | solution.py:13
  231.0 68.2 %all-gather.23.cloned.1.call-done = bf16[1,4096,1024]{2,1,0:T(8,128)(2,1)} async-done(((bf16[1,128,1024]{2,1,0:T(8,128)(2,1)}), bf16[1,4096,1024]{2,1,0:T(8,128)(2,1)}) %all-gather.23.cloned.1.call-update) | async-done | bytes 8388624 | tf_op jit(solution)/shard_map/all_gather | solution.py:148
  299.3 27.7 %fusion.286 = (f32[512]{0:T(512)S(1)}, f32[512,1024]{1,0:T(8,128)S(1)}, f32[512,1024]{1,0:T(8,128)}) fusion(f32[1024]{0:T(1024)S(1)} %bitcast.245, f32[1024]{0:T(1024)S(1)} %bitcast.256, f32[1024]{0:T(1024)S(1)} %bitcast.213, f32[512]{0:T(512)S(1)} %add_rsqrt_fusion.3, f32[512,1024]{1,0:T(8,128)S(1)} %get-tuple-element.57, ...), kind=kOutput, calls=%fused_computation.373 | convolution fusion | flops 4437048832 | bytes 23103488 | tf_op jit(solution)/shard_map/dot_general | solution.py:13
  328.7 41.2 %all-gather.25.cloned.1.call-done = bf16[1,1024,3072]{2,1,0:T(8,128)(2,1)} async-done(((bf16[1,32,3072]{2,1,0:T(8,128)(2,1)}), bf16[1,1024,3072]{2,1,0:T(8,128)(2,1)}) %all-gather.25.cloned.1.call-update) | async-done | bytes 6291472 | tf_op jit(solution)/shard_map/all_gather | solution.py:145
  397.1 8.6 %fusion.189 = bf16[16,64,512]{2,1,0:T(8,128)(2,1)} fusion(bf16[512,16,64]{0,2,1:T(8,128)(2,1)S(1)} %bitcast.201, f32[16,512,512]{1,2,0:T(8,128)} %get-tuple-element.96, f32[16,512]{1,0:T(8,128)S(1)} %fusion.1, f32[16,512]{1,0:T(8,128)S(1)} %get-tuple-element.95), kind=kOutput, calls=%fused_computation.247 | convolution fusion | flops 549978112 | bytes 18939904 | tf_op jit(solution)/shard_map/hqk,khd->qhd/dot_general | solution.py:79
  405.7 21.9 %all-gather.27.cloned.1.call-done = bf16[1,1024,1024]{2,1,0:T(8,128)(2,1)} async-done(((bf16[1,32,1024]{2,1,0:T(8,128)(2,1)}), bf16[1,1024,1024]{2,1,0:T(8,128)(2,1)}) %all-gather.27.cloned.1.call-update) | async-done | bytes 2097168 | tf_op jit(solution)/shard_map/all_gather | solution.py:146
  434.2 72.3 %all-gather.29.cloned.1.call-done = bf16[1,1024,4096]{2,1,0:T(8,128)(2,1)} async-done(((bf16[1,32,4096]{2,1,0:T(8,128)(2,1)}), bf16[1,1024,4096]{2,1,0:T(8,128)(2,1)}) %all-gather.29.cloned.1.call-update) | async-done | bytes 8388624 | tf_op jit(solution)/shard_map/all_gather | solution.py:147
  506.5 12.1 %fusion.30 = f32[512,4096]{1,0:T(8,128)} fusion(bf16[1,1024,4096]{2,1,0:T(8,128)(2,1)} %all-gather.29.cloned.1.call-done, f32[512,1024]{1,0:T(8,128)} %copy-done.17, f32[1024]{0:T(1024)S(1)} %bitcast.253, f32[1024]{0:T(1024)S(1)} %bitcast.220, f32[512]{0:T(512)S(1)} %add_rsqrt_fusion.1, f32[512]{0:T(512)S(1)} %broadcast_multiply_fusion.9), kind=kOutput, calls=%fused_computation.44 | convolution fusion | flops 4297588736 | bytes 18886656 | tf_op jit(solution)/shard_map/dot_general | solution.py:13
  518.6 66.6 %all-gather.31.cloned.1.call-done = bf16[1,4096,1024]{2,1,0:T(8,128)(2,1)} async-done(((bf16[1,128,1024]{2,1,0:T(8,128)(2,1)}), bf16[1,4096,1024]{2,1,0:T(8,128)(2,1)}) %all-gather.31.cloned.1.call-update) | async-done | bytes 8388624 | tf_op jit(solution)/shard_map/all_gather | solution.py:148
  585.2 27.8 %fusion.284 = (f32[512]{0:T(512)S(1)}, f32[512,1024]{1,0:T(8,128)S(1)}, f32[512,1024]{1,0:T(8,128)}) fusion(f32[1024]{0:T(1024)S(1)} %bitcast.243, f32[1024]{0:T(1024)S(1)} %bitcast.254, f32[1024]{0:T(1024)S(1)} %bitcast.221, f32[512]{0:T(512)S(1)} %add_rsqrt_fusion.1, f32[512,1024]{1,0:T(8,128)S(1)} %copy-done.18, f32[512]{0:T(512)S(1)} %broadcast_multiply_fusion.9, ...), kind=kOutput, calls=%fused_computation.371 | convolution fusion | flops 4437048832 | bytes 23103488 | tf_op jit(solution)/shard_map/dot_general | solution.py:13
  616.3 12.9 %fusion.301 = (f32[4096]{0:T(1024)}, bf16[512,4096]{1,0:T(8,128)(2,1)}) fusion(f32[512,4096]{1,0:T(8,128)} %fusion.30, f32[4096]{0:T(1024)S(1)} %bitcast.237, bf16[1,4096,1024]{2,1,0:T(8,128)(2,1)} %all-gather.31.cloned.1.call-done, f32[512,1024]{1,0:T(8,128)S(1)} %get-tuple-element.45), kind=kOutput, calls=%fused_computation.388 | convolution fusion | flops 4320653312 | bytes 23101440 | tf_op jit(solution)/shard_map/dot_general | solution.py:17
  641.6 10.4 %bitcast_convert_fusion.2 = (bf16[512,16,64]{0,2,1:T(8,128)(2,1)}, f32[16,64,512]{2,1,0:T(8,128)}) fusion(bf16[512,16,64]{0,2,1:T(8,128)(2,1)S(1)} %bitcast.195, f32[16,512,512]{1,2,0:T(8,128)} %get-tuple-element.96, f32[16,512]{1,0:T(8,128)S(1)} %log_add_fusion.1), kind=kOutput, calls=%fused_computation.198 | convolution fusion | flops 545783808 | bytes 21004288 | tf_op jit(solution)/shard_map/hqk,qhd->khd/dot_general | solution.py:95
  652.0 13.8 %multiply_reduce_fusion.1 = (f32[16,512]{1,0:T(8,128)}, f32[16,512,512]{1,2,0:T(8,128)}) fusion(f32[16,512,512]{1,2,0:T(8,128)} %get-tuple-element.96, f32[16,512]{1,0:T(8,128)} %copy-done.29, bf16[512,16,64]{0,2,1:T(8,128)(2,1)S(1)} %bitcast.196, bf16[512,16,64]{0,2,1:T(8,128)(2,1)} %bitcast.202), kind=kOutput, calls=%fused_computation.4 | convolution fusion | flops 549445632 | bytes 35717120 | tf_op jit(solution)/shard_map/qhd,khd->hqk/dot_general | solution.py:92
  665.9 10.7 %multiply_convert_fusion.1 = bf16[16,512,512]{1,2,0:T(8,128)(2,1)} fusion(f32[16,512,512]{1,2,0:T(8,128)} %get-tuple-element.103, f32[16,512,512]{1,2,0:T(8,128)S(1)} %bitcast.186, f32[16,512]{1,0:T(8,128)} %get-tuple-element.102, f32[16,512]{1,0:T(8,128)} %copy-done.29), kind=kLoop, calls=%fused_computation.3 | loop fusion | flops 16777216 | bytes 42008576 | tf_op jit(solution)/shard_map/convert_element_type | solution.py:99
  687.1 11.5 %fusion.146 = (f32[]{:T(128)}, f32[]{:T(128)}, f32[]{:T(128)}, f32[1024]{0:T(1024)}, f32[512]{0:T(512)S(1)}, /*index=5*/f32[512]{0:T(512)S(1)}, f32[]{:T(128)}, f32[]{:T(128)}, f32[]{:T(128)}, f32[512,1024]{1,0:T(8,128)S(1)}) fusion(bf16[512,1024]{1,0:T(8,128)(2,1)S(1)} %copy-done.71, f32[512]{0:T(512)S(1)} %copy-done.31, f32[512,1024]{1,0:T(8,128)S(1)} %copy-done.72, ...), kind=kOutput, calls=%fused_computation.177 | convolution fusion | flops 3247962112 | bytes 25204760 | tf_op jit(solution)/shard_map/dot_general | solution.py:17
  699.3 11.9 %fusion.302 = (f32[4096]{0:T(1024)}, bf16[512,4096]{1,0:T(8,128)(2,1)S(1)}) fusion(f32[512,4096]{1,0:T(8,128)} %fusion.38, f32[4096]{0:T(1024)S(1)} %bitcast.234, bf16[1,4096,1024]{2,1,0:T(8,128)(2,1)} %all-gather.23.cloned.1.call-done, f32[512,1024]{1,0:T(8,128)S(1)} %get-tuple-element.43), kind=kOutput, calls=%fused_computation.389 | convolution fusion | flops 4320653312 | bytes 23101440 | tf_op jit(solution)/shard_map/dot_general | solution.py:17
  723.7 10.3 %bitcast_convert_fusion = (bf16[512,16,64]{0,2,1:T(8,128)(2,1)}, f32[16,64,512]{2,1,0:T(8,128)}) fusion(bf16[512,16,64]{0,2,1:T(8,128)(2,1)S(1)} %bitcast.197, f32[16,512,512]{1,2,0:T(8,128)} %get-tuple-element.92, f32[16,512]{1,0:T(8,128)S(1)} %copy-done.28), kind=kOutput, calls=%fused_computation.194 | convolution fusion | flops 545783808 | bytes 21004288 | tf_op jit(solution)/shard_map/hqk,qhd->khd/dot_general | solution.py:95
  734.0 13.9 %multiply_reduce_fusion = (f32[16,512]{1,0:T(8,128)}, f32[16,512,512]{1,2,0:T(8,128)}) fusion(f32[16,512,512]{1,2,0:T(8,128)} %get-tuple-element.92, f32[16,512]{1,0:T(8,128)} %log_add_fusion, bf16[512,16,64]{0,2,1:T(8,128)(2,1)S(1)} %bitcast.198, bf16[512,16,64]{0,2,1:T(8,128)(2,1)} %bitcast.200), kind=kOutput, calls=%fused_computation.1 | convolution fusion | flops 549445632 | bytes 35717120 | tf_op jit(solution)/shard_map/qhd,khd->hqk/dot_general | solution.py:92
  748.0 10.8 %multiply_convert_fusion = bf16[16,512,512]{1,2,0:T(8,128)(2,1)} fusion(f32[16,512,512]{1,2,0:T(8,128)} %get-tuple-element.111, f32[16,512,512]{1,2,0:T(8,128)S(1)} %bitcast.184, f32[16,512]{1,0:T(8,128)} %get-tuple-element.110, f32[16,512]{1,0:T(8,128)} %log_add_fusion), kind=kLoop, calls=%fused_computation | loop fusion | flops 16777216 | bytes 42008576 | tf_op jit(solution)/shard_map/convert_element_type | solution.py:99
  777.2 40.9 %all-reduce.2 = (f32[1,2,1024]{2,1,0:T(2,128)S(1)}, f32[1,2,1024]{2,1,0:T(2,128)S(1)}, f32[1,1024]{1,0:T(1,128)S(1)}, f32[1,1024]{1,0:T(1,128)S(1)}, f32[1,2,102...) all-reduce(f32[1,2,1024]{2,1,0:T(2,128)S(1)} %maximum_bitcast_fusio, ...), channel_id=1, replica_groups=mesh['dp'=8,'shard'=4] {'dp','shard'}, use_global_device_ids=true, to_apply=%region_27.28 | all-reduce | flops 20487 | bytes 163896 | tf_op jit(solution)/shard_map/psum | solution.py:237
  822.4 8.8 %fusion.169 = f32[512,1024]{1,0:T(8,128)} fusion(f32[512,1024]{1,0:T(8,128)} %copy-done.24, bf16[1,1024,3072]{2,1,0:T(8,128)(2,1)} %all-gather.17.cloned.1.call-done, bf16[512,1024]{0,1:T(8,128)(2,1)} %bitcast.205, bf16[512,1024]{0,1:T(8,128)(2,1)} %bitcast.206, bf16[512,1024]{0,1:T(8,128)(2,1)S(1)} %bitcast.203), kind=kOutput, calls=%fused_computation.243 | convolution fusion | flops 3231186944 | bytes 13631488 | tf_op jit(solution)/shard_map/dot_general | solution.py:17
  (276 shorter events, 159.1 us)
Async XLA Ops:
  7.2 76.3 %all-gather.17.cloned.1.call-start = ((), (), s32[]{:S(2)}) async-start(), calls=%async_computation | async-start | bytes 6488064 | tf_op jit(solution)/shard_map/all_gather | solution.py:145
  9.0 132.8 %all-gather.19.cloned.1.call-start = ((), (), s32[]{:S(2)}) async-start(), calls=%async_computation.1 | async-start | bytes 2162688 | tf_op jit(solution)/shard_map/all_gather | solution.py:146
  10.6 210.1 %all-gather.21.cloned.1.call-start = ((), (), s32[]{:S(2)}) async-start(), calls=%async_computation.2 | async-start | bytes 8650752 | tf_op jit(solution)/shard_map/all_gather | solution.py:147
  12.6 286.7 %all-gather.23.cloned.1.call-start = ((), (), s32[]{:S(2)}) async-start(), calls=%async_computation.3 | async-start | bytes 8650752 | tf_op jit(solution)/shard_map/all_gather | solution.py:148
  14.5 355.4 %all-gather.25.cloned.1.call-start = ((), (), s32[]{:S(2)}) async-start(), calls=%async_computation.4 | async-start | bytes 6488064 | tf_op jit(solution)/shard_map/all_gather | solution.py:145
  15.1 412.5 %all-gather.27.cloned.1.call-start = ((), (), s32[]{:S(2)}) async-start(), calls=%async_computation.5 | async-start | bytes 2162688 | tf_op jit(solution)/shard_map/all_gather | solution.py:146
  15.7 490.8 %all-gather.29.cloned.1.call-start = ((), (), s32[]{:S(2)}) async-start(), calls=%async_computation.6 | async-start | bytes 8650752 | tf_op jit(solution)/shard_map/all_gather | solution.py:147
  16.5 568.7 %all-gather.31.cloned.1.call-start = ((), (), s32[]{:S(2)}) async-start(), calls=%async_computation.7 | async-start | bytes 8650752 | tf_op jit(solution)/shard_map/all_gather | solution.py:148
  24.4 117.5 %copy-start.57 = (f32[1,1024]{1,0:T(1,128)}, f32[1,1024]{1,0:T(1,128)S(1)}, u32[]{:S(2)}) copy-start(f32[1,1024]{1,0:T(1,128)S(1)} %get-tuple-element.88) | copy-start | bytes 12292
  25.8 273.5 %copy-start.61 = (f32[1,1024]{1,0:T(1,128)}, f32[1,1024]{1,0:T(1,128)S(1)}, u32[]{:S(2)}) copy-start(f32[1,1024]{1,0:T(1,128)S(1)} %get-tuple-element.86) | copy-start | bytes 12292
  27.1 272.1 %copy-start.36 = (f32[1,1,1024]{2,1,0:T(1,128)}, f32[1,1,1024]{2,1,0:T(1,128)S(1)}, u32[]{:S(2)}) copy-start(f32[1,1,1024]{2,1,0:T(1,128)S(1)} %get-tuple-element.75) | copy-start | bytes 12292
  31.4 267.9 %copy-start.46 = (f32[1,4096]{1,0:T(1,128)}, f32[1,4096]{1,0:T(1,128)S(1)}, u32[]{:S(2)}) copy-start(f32[1,4096]{1,0:T(1,128)S(1)} %get-tuple-element.72) | copy-start | bytes 49156
  146.7 152.6 %copy-start.11 = (f32[512,1024]{1,0:T(8,128)}, f32[512,1024]{1,0:T(8,128)S(1)}, u32[]{:S(2)}) copy-start(f32[512,1024]{1,0:T(8,128)S(1)} %get-tuple-element.57) | copy-start | bytes 6291460
  146.7 152.6 %copy-start.32 = (f32[512]{0:T(512)}, f32[512]{0:T(512)S(1)}, u32[]{:S(2)}) copy-start(f32[512]{0:T(512)S(1)} %broadcast_multiply_fusion.11) | copy-start | bytes 6148
  147.0 152.3 %copy-start.51 = (f32[512]{0:T(512)}, f32[512]{0:T(512)S(1)}, u32[]{:S(2)}) copy-start(f32[512]{0:T(512)S(1)} %add_rsqrt_fusion.3) | copy-start | bytes 6148
  299.3 70.6 %copy-start.38 = (f32[1,1,1024]{2,1,0:T(1,128)S(1)}, f32[1,1,1024]{2,1,0:T(1,128)}, u32[]{:S(2)}) copy-start(f32[1,1,1024]{2,1,0:T(1,128)} %get-tuple-element.74) | copy-start | bytes 12292
  327.0 100.6 %copy-start.34 = (f32[512]{0:T(512)}, f32[512]{0:T(512)S(1)}, u32[]{:S(2)}) copy-start(f32[512]{0:T(512)S(1)} %broadcast_multiply_fusion.10) | copy-start | bytes 6148
  328.7 98.9 %copy-start.53 = (f32[512]{0:T(512)}, f32[512]{0:T(512)S(1)}, u32[]{:S(2)}) copy-start(f32[512]{0:T(512)S(1)} %add_rsqrt_fusion.2) | copy-start | bytes 6148
  427.6 78.9 %copy-start.40 = (f32[1,1,1024]{2,1,0:T(1,128)S(1)}, f32[1,1,1024]{2,1,0:T(1,128)}, u32[]{:S(2)}) copy-start(f32[1,1,1024]{2,1,0:T(1,128)} %get-tuple-element.76) | copy-start | bytes 12292
  427.6 78.9 %copy-start.68 = (f32[1,1,1024]{2,1,0:T(1,128)S(1)}, f32[1,1,1024]{2,1,0:T(1,128)}, u32[]{:S(2)}) copy-start(f32[1,1,1024]{2,1,0:T(1,128)} %get-tuple-element.80) | copy-start | bytes 12292
  434.2 207.4 %copy-start.29 = (f32[16,512]{1,0:T(8,128)}, f32[16,512]{1,0:T(8,128)S(1)}, u32[]{:S(2)}) copy-start(f32[16,512]{1,0:T(8,128)S(1)} %log_add_fusion.1) | copy-start | bytes 98308
  506.5 78.6 %copy-start.18 = (f32[512,1024]{1,0:T(8,128)S(1)}, f32[512,1024]{1,0:T(8,128)}, u32[]{:S(2)}) copy-start(f32[512,1024]{1,0:T(8,128)} %copy-done.17) | copy-start | bytes 6291460
  506.5 78.6 %copy-start.49 = (f32[1,4096]{1,0:T(1,128)S(1)}, f32[1,4096]{1,0:T(1,128)}, u32[]{:S(2)}) copy-start(f32[1,4096]{1,0:T(1,128)} %get-tuple-element.71) | copy-start | bytes 49156
  506.5 78.6 %copy-start.59 = (f32[1,1024]{1,0:T(1,128)S(1)}, f32[1,1024]{1,0:T(1,128)}, u32[]{:S(2)}) copy-start(f32[1,1024]{1,0:T(1,128)} %get-tuple-element.85) | copy-start | bytes 12292
  (67 other events, 788.4 us)
Sparse Core Ops, SparseCore 0:
  11.4 71.9 all-gather.16
  86.9 54.8 all-gather.18
  144.8 75.9 all-gather.20
  223.5 75.6 all-gather.22
  302.0 67.8 all-gather.24
  372.7 54.8 all-gather.26
  430.6 75.9 all-gather.28
  509.4 75.6 all-gather.30
where the time goes:
time: 848 us; the launch traced here: 838 us
  waiting for transfers between devices  421 us (50%)
  matrix products  263 us (31%)
  other arithmetic  63.6 us (8%)
  blocking collectives  40.9 us (5%)
  local copies, waits for them, and re-layouts  31.4 us (4%)
  between operations  17.9 us (2%)
    all_gather x2, waiting for transfers between devices, local(): lax.all_gather(w_up[layer_at], ('dp', 'shard'), axis=0, tiled=True)  146 us
    all_gather x2, waiting for transfers between devices, local(): lax.all_gather(w_down[layer_at], ('dp', 'shard'), axis=0, tiled=True)  135 us
    dot_general x8, matrix products, mat_dot(): return jnp.dot(left_side, right_side, preferred_element_type=jnp.float32)  99.7 us
    all_gather x2, waiting for transfers between devices, local(): lax.all_gather(w_qkv[layer_at], ('dp', 'shard'), axis=0, tiled=True)  93.1 us
    dot_general x8, matrix products, back_dot(): lax.dot_general(left_side, right_side, (((1,), (1,)), ((), ())), preferre...  63.7 us
    all_gather x2, waiting for transfers between devices, local(): lax.all_gather(w_out[layer_at], ('dp', 'shard'), axis=0, tiled=True)  45 us
    psum x1, blocking collectives, local(): lax.psum((layer_terms[0], layer_terms[1], layer_terms[2], layer_terms[3],...  40.9 us
    dot_general x2, matrix products, attend_back(): jnp.einsum('qhd,khd->hqk', grad_heads, split_heads(values_part), preferre...  27.7 us
  transfers between devices with their start and end apart: 8, of which 8 were waited for; matrix products, arithmetic and copies ran while one was open for 18% of the time, Pallas kernels for 0%

commit v1 on v0

v1 whole, which is shorter than its diff:
```python
import functools
import jax
import jax.numpy as jnp
from jax import lax
from jax.experimental import pallas as pl
from jax.experimental.pallas import tpu as pltpu
from jax.sharding import PartitionSpec as P

BF = jnp.bfloat16
F32 = jnp.float32


def nt(a, b):
    return lax.dot_general(a, b, (((1,), (1,)), ((), ())), preferred_element_type=F32)


def nn(a, b):
    return lax.dot_general(a, b, (((1,), (0,)), ((), ())), preferred_element_type=F32)


def tn(a, b):
    return lax.dot_general(a, b, (((0,), (0,)), ((), ())), preferred_element_type=F32)


def fold8(t):
    return jnp.sum(t.reshape(t.shape[0] // 8, 8, t.shape[1]), axis=0)


class Ring:
    def __init__(self, buf, sem, segments):
        self.buf, self.sem, self.segments = buf, sem, segments
        self.slots, self.rows = buf.shape[0], buf.shape[1]
        self.base = 0

    def fetch(self, at):
        slot = lax.rem(at, self.slots)
        first = 0
        for ref, count in self.segments:
            if isinstance(at, int):
                if first <= at < first + count:
                    row = (at - first) * self.rows
                    pltpu.make_async_copy(ref.at[pl.ds(row, self.rows)], self.buf.at[slot], self.sem.at[slot]).start()
            else:

                @pl.when(jnp.logical_and(at >= first, at < first + count))
                def _(ref=ref, first=first):
                    row = pl.multiple_of((at - first) * self.rows, self.rows)
                    pltpu.make_async_copy(ref.at[pl.ds(row, self.rows)], self.buf.at[slot], self.sem.at[slot]).start()

            first += count

    def prime(self):
        for at in range(self.slots):
            self.fetch(at)

    def run(self, count, body):
        base = self.base

        def step(j, carry):
            at = base + j
            slot = lax.rem(at, self.slots)
            pltpu.make_async_copy(self.segments[0][0].at[pl.ds(0, self.rows)], self.buf.at[slot], self.sem.at[slot]).wait()
            body(j, self.buf[slot])
            self.fetch(at + self.slots)
            return carry

        lax.fori_loop(0, count, step, 0)
        self.base = base + count


def backward_kernel(layers, *refs):
    cot, valid, gain = refs[:3]
    kept = [refs[3 + at * layers : 3 + (at + 1) * layers] for at in range(13)]
    q, k, v, pt, slope, n1, n2, r1, r2, wqkv, wout, wup, wdown = kept
    backward_body(layers, cot, valid, gain, q, k, v, pt, slope, n1, n2, r1, r2, wqkv, wout, wup, wdown, *refs[3 + 13 * layers :])


def backward_body(
    layers, cot, valid, gain, q, k, v, pt, slope, n1, n2, r1, r2, wqkv, wout, wup, wdown,
    dh_out, grads,
    e_buf, x_buf, z_buf, du_buf, dp_buf, do_buf, cot_buf,
    q_buf, k_buf, v_buf, pt_buf, sl_buf, n1_buf, n2_buf,
    ring_a, ring_b, ring_c, sem_a, sem_b, sem_c, sem_in, sem_out,
):
    slots, width = e_buf.shape
    ff = du_buf.shape[1]
    heads = pt[0].shape[0]
    hd = width // heads
    half = slots // 2
    scale = hd ** (-0.5)
    order = list(reversed(range(layers)))

    sources = (n2, slope, n1, q, k, v, pt)
    buffers = (n2_buf, sl_buf, n1_buf, q_buf, k_buf, v_buf, pt_buf)

    def load(which, layer, par):
        return pltpu.make_async_copy(sources[which][layer], buffers[which].at[par], sem_in.at[par, which])

    cot_copy = pltpu.make_async_copy(cot, cot_buf, sem_out.at[0])
    cot_copy.start()
    load(0, order[0], 0).start()
    seg_a = []
    seg_b = []
    seg_c = []
    for l in order:
        seg_a += [(wdown[l], ff // ring_a.shape[1]), (wout[l], width // ring_a.shape[1])]
        seg_b += [(wup[l], width // ring_b.shape[1])]
        seg_c += [(wqkv[l], width // ring_c.shape[1])]
    ra, rb, rc = Ring(ring_a, sem_a, seg_a), Ring(ring_b, sem_b, seg_b), Ring(ring_c, sem_c, seg_c)
    ra.prime()
    load(1, order[0], 0).start()
    rb.prime()
    for which in range(2, 7):
        load(which, order[0], 0).start()
    rc.prime()
    for which in range(7):
        for step, l in enumerate(order[1:], 1):
            if step < 2:
                load(which, l, step).start()

    chunk = 32
    cot_copy.wait()

    def mask_cot(c, carry):
        rows = pl.ds(pl.multiple_of(c * chunk, chunk), chunk)
        e_buf[rows, :] = cot_buf[rows, :].astype(F32) * valid[rows, :]
        return carry

    lax.fori_loop(0, slots // chunk, mask_cot, 0)

    def norm_back(src, dst, gain_row, n_ref, r_ref):
        def step(c, carry):
            s_in, s_out = carry
            rows = pl.ds(pl.multiple_of(c * chunk, chunk), chunk)
            g = src[rows, :]
            n = n_ref[rows, :].astype(F32)
            ge = g * gain_row
            m1 = jnp.mean(ge, axis=1, keepdims=True)
            m2 = jnp.mean(ge * n, axis=1, keepdims=True)
            dz = r_ref[rows, :] * (ge - m1 - n * m2)
            dst[rows, :] = dz
            z_buf[rows, :] = dz.astype(BF)
            return (s_in + fold8(g), s_out + fold8(dz))

        zero = jnp.zeros((8, width), F32)
        s_in, s_out = lax.fori_loop(0, slots // chunk, step, (zero, zero))
        return jnp.sum(s_in, axis=0, keepdims=True), jnp.sum(s_out, axis=0, keepdims=True)

    for step, l in enumerate(order):
        par = step % 2

        load(0, l, par).wait()
        s_in, s_out = norm_back(e_buf, x_buf, gain[l, 1:2, :], n2_buf.at[par], r2[l])
        grads[l, 4:5, :] = s_in
        grads[l, 9:10, :] = s_out

        load(1, l, par).wait()
        wide = ring_a.shape[1]

        def down_body(j, w):
            cols = pl.ds(pl.multiple_of(j * wide, wide), wide)
            du = nt(z_buf[...], w) * sl_buf[par, :, cols].astype(F32)
            du_buf[:, cols] = du.astype(BF)
            part = jnp.sum(fold8(du), axis=0, keepdims=True)
            per = width // wide
            grads[l, pl.ds(5 + j // per, 1), pl.ds(pl.multiple_of(lax.rem(j, per) * wide, wide), wide)] = part

        ra.run(ff // wide, down_body)
        nb = ring_b.shape[1]

        def up_body(j, w):
            cols = pl.ds(pl.multiple_of(j * nb, nb), nb)
            x_buf[:, cols] = x_buf[:, cols] + nt(du_buf[...], w)

        rb.run(width // nb, up_body)

        load(2, l, par).wait()
        s_in, s_out = norm_back(x_buf, x_buf, gain[l, 0:1, :], n1_buf.at[par], r1[l])
        grads[l, 3:4, :] = s_in
        grads[l, 2:3, :] = s_out

        def out_body(j, w):
            cols = pl.ds(pl.multiple_of(j * wide, wide), wide)
            do_buf[:, cols] = nt(z_buf[...], w).astype(BF)

        ra.run(width // wide, out_body)

        for which in range(3, 7):
            load(which, l, par).wait()
        lane = lax.broadcasted_iota(jnp.int32, (1, 2 * hd), 1)
        sides = (lane < hd, lane >= hd)

        def pair(hp, carry):
            cols = pl.ds(pl.multiple_of(hp * 2 * hd, 2 * hd), 2 * hd)
            sum_q = jnp.zeros((8, 2 * hd), F32)
            sum_v = jnp.zeros((8, 2 * hd), F32)
            for b in range(2):
                rows = pl.ds(b * half, half)
                q2, k2, v2, do2 = (r[rows, cols] for r in (q_buf.at[par], k_buf.at[par], v_buf.at[par], do_buf))
                dq = dk = dv = None
                for side in range(2):
                    keep = sides[side]
                    zero = jnp.zeros_like(q2)
                    pb = pt_buf[par, 2 * hp + side, b]
                    dpt = nt(jnp.where(keep, v2, zero), do2)
                    p32 = pb.astype(F32)
                    t = p32 * dpt
                    inner = jnp.sum(fold8(t), axis=0, keepdims=True)
                    ds = (t - p32 * inner).astype(BF)
                    a_v = nn(pb, jnp.where(keep, do2, zero))
                    a_k = nn(ds, jnp.where(keep, q2, zero))
                    a_q = tn(ds, jnp.where(keep, k2, zero))
                    dv = a_v if dv is None else dv + a_v
                    dk = a_k if dk is None else dk + a_k
                    dq = a_q if dq is None else dq + a_q
                dq = dq * scale
                dk = dk * scale
                dp_buf[rows, cols] = dq.astype(BF)
                dp_buf[rows, pl.ds(pl.multiple_of(width + hp * 2 * hd, 2 * hd), 2 * hd)] = dk.astype(BF)
                dp_buf[rows, pl.ds(pl.multiple_of(2 * width + hp * 2 * hd, 2 * hd), 2 * hd)] = dv.astype(BF)
                sum_q = sum_q + fold8(dq)
                sum_v = sum_v + fold8(dv)
            grads[l, 0:1, cols] = jnp.sum(sum_q, axis=0, keepdims=True)
            grads[l, 1:2, cols] = jnp.sum(sum_v, axis=0, keepdims=True)
            return carry

        lax.fori_loop(0, heads // 2, pair, 0)
        nc = ring_c.shape[1]
        last = step == layers - 1

        def qkv_body(j, w):
            cols = pl.ds(pl.multiple_of(j * nc, nc), nc)
            e_buf[:, cols] = x_buf[:, cols] + nt(dp_buf[...], w)
            if last:
                pltpu.make_async_copy(e_buf.at[:, cols], dh_out.at[:, cols], sem_out.at[0]).start()

        rc.run(width // nc, qkv_body)
        for which in range(7):
            if step + 2 < layers:
                load(which, order[step + 2], par).start()
        grads[l, 10:16, :] = jnp.zeros((6, width), F32)

    for j in range(width // nc):
        cols = pl.ds(j * nc, nc)
        pltpu.make_async_copy(e_buf.at[:, cols], dh_out.at[:, cols], sem_out.at[0]).wait()


def backward(cot, valid, gain, kept):
    slots, width = cot.shape
    layers = len(kept[0])
    ff = kept[4][0].shape[1]
    heads = kept[3][0].shape[0]
    half = slots // 2
    hbm = pl.BlockSpec(memory_space=pl.ANY)
    vm = pl.BlockSpec(memory_space=pltpu.VMEM)
    ta, tb, tc = min(512, width), min(256, width), min(256, width)
    return pl.pallas_call(
        functools.partial(backward_kernel, layers),
        out_shape=(
            jax.ShapeDtypeStruct((slots, width), F32),
            jax.ShapeDtypeStruct((layers, 16, width), F32),
        ),
        in_specs=[hbm, vm, vm] + [hbm] * (7 * layers) + [vm] * (2 * layers) + [hbm] * (4 * layers),
        out_specs=(hbm, vm),
        scratch_shapes=[
            pltpu.VMEM((slots, width), F32),
            pltpu.VMEM((slots, width), F32),
            pltpu.VMEM((slots, width), BF),
            pltpu.VMEM((slots, ff), BF),
            pltpu.VMEM((slots, 3 * width), BF),
            pltpu.VMEM((slots, width), BF),
            pltpu.VMEM((slots, width), BF),
        ]
        + [pltpu.VMEM((2, slots, width), BF)] * 3
        + [
            pltpu.VMEM((2, heads, 2, half, half), BF),
            pltpu.VMEM((2, slots, ff), BF),
            pltpu.VMEM((2, slots, width), BF),
            pltpu.VMEM((2, slots, width), BF),
            pltpu.VMEM((3, ta, width), BF),
            pltpu.VMEM((2, tb, ff), BF),
            pltpu.VMEM((2, tc, 3 * width), BF),
            pltpu.SemaphoreType.DMA((3,)),
            pltpu.SemaphoreType.DMA((2,)),
            pltpu.SemaphoreType.DMA((2,)),
            pltpu.SemaphoreType.DMA((2, 7)),
            pltpu.SemaphoreType.DMA((1,)),
        ],
        compiler_params=pltpu.CompilerParams(vmem_limit_bytes=67000000),
        name="backward",
    )(cot, valid, gain, *[a for one in kept for a in one])


HEADS = 16
AXES = ("dp", "shard")


def normalize(stream, gain_row, shift_row):
    mean_row = jnp.mean(stream, axis=-1, keepdims=True)
    centred = stream - mean_row
    variance = jnp.mean(centred * centred, axis=-1, keepdims=True)
    inv_std = lax.rsqrt(variance + 1e-06)
    normed = centred * inv_std
    return normed * gain_row + shift_row, normed, inv_std


def local(
    tokens, lengths, w_qkv, w_out, w_up, w_down, ln_gain, bias_qv, bias_out, ln_bias, bias_up, bias_down, cotangent
):
    slots, width = tokens.shape
    layers = w_qkv.shape[0]
    half = slots // 2
    hd = width // HEADS
    first, second = lengths[0, 0], lengths[0, 1]
    shift = jnp.where(first == half, 0, first)
    place = lax.rem(jnp.arange(slots, dtype=jnp.int32) + shift, slots)
    valid = place < first + second
    same = valid.reshape(2, half)[:, :, None] == valid.reshape(2, half)[:, None, :]
    valid = valid.astype(F32)[:, None]

    def turn(a, by):
        return lax.dynamic_slice_in_dim(jnp.concatenate([a, a], axis=0), by, slots, axis=0)

    stream = turn(tokens, shift).astype(F32)
    cot = turn(cotangent, shift)
    full = [[lax.all_gather(w[l], AXES, axis=0, tiled=True) for w in (w_qkv, w_out, w_up, w_down)] for l in range(layers)]
    kept = []
    squares = []
    for l in range(layers):
        mat_qkv, mat_out, mat_up, mat_down = full[l]
        projected = nn(stream.astype(BF), mat_qkv)
        q = (projected[:, :width] + bias_qv[l, 0]).astype(BF)
        k = projected[:, width : 2 * width].astype(BF)
        v = (projected[:, 2 * width :] + bias_qv[l, 1]).astype(BF)
        q4, k4, v4 = (a.reshape(2, half, HEADS, hd) for a in (q, k, v))
        st = jnp.einsum("bqhd,bkhd->hbkq", q4, k4, preferred_element_type=F32) * hd ** (-0.5)
        st = jnp.where(same[None], st, -1e30)
        ex = jnp.exp(st - jnp.max(st, axis=2, keepdims=True))
        pt = (ex / jnp.sum(ex, axis=2, keepdims=True)).astype(BF)
        mixed = jnp.einsum("hbkq,bkhd->bqhd", pt, v4, preferred_element_type=F32).reshape(slots, width).astype(BF)
        branch = nn(mixed, mat_out) + bias_out[l]
        x1, n1, r1 = normalize(stream + branch, ln_gain[l, 0], ln_bias[l, 0])
        u = nn(x1.astype(BF), mat_up) + bias_up[l]
        phi = 0.5 * (1.0 + lax.erf(u * 0.7071067811865476))
        slope = (phi + u * (jnp.exp(-0.5 * u * u) * 0.3989422804014327)).astype(BF)
        ffn = nn((u * phi).astype(BF), mat_down) + bias_down[l]
        nxt, n2, r2 = normalize(x1 + ffn, ln_gain[l, 1], ln_bias[l, 1])
        squares.append(jnp.stack([jnp.sum(valid * a * a) for a in (stream, branch, ffn)]))
        kept.append((q, k, v, pt, slope, n1.astype(BF), n2.astype(BF), r1, r2))
        stream = nxt
    dh, grads = backward(cot, valid, ln_gain, list(zip(*kept)) + list(zip(*full)))
    count = jnp.sum(lengths).astype(F32)
    grads, squares, count = lax.psum((grads[:, :10], jnp.stack(squares), count), AXES)
    back = lax.rem(slots - shift, slots)
    return (
        turn(stream.astype(BF), back),
        turn(dh, back),
        grads[:, 0:2],
        grads[:, 2],
        grads[:, 3:5],
        grads[:, 5:9].reshape(layers, -1),
        grads[:, 9],
        jnp.sqrt(squares / (count * width)),
    )


def solution(mesh):
    rows = P(AXES, None)
    weight = P(None, AXES, None)
    in_specs = (rows, rows, weight, weight, weight, weight, P(), P(), P(), P(), P(), P(), rows)
    return jax.shard_map(
        local, mesh=mesh, in_specs=in_specs, out_specs=(rows, rows, P(), P(), P(), P(), P(), P()), check_vma=False
    )
```

time: 848 us -> 830 us (0.979)
  matrix products: 263 us -> 79.9 us
  waiting for transfers between devices: 421 us -> 537 us
  Pallas kernels: 0 us -> 74.8 us
  other arithmetic: 63.6 us -> 33.9 us
    dot_general x28 -> x12, matrix products: 263 us -> 79.9 us  [the longest x8 69.7 us: nn(): lax.dot_general(a, b, (((1,), (0,)), ((), ())), preferred_element_type=F32)]
    psum x0 -> x1, waiting for transfers between devices: none -> 76.4 us  [local(): lax.psum((grads[:, :10], jnp.stack(squares), count), AXES)]
    pallas_call x0 -> x1, Pallas kernels: none -> 74.8 us  [backward(): pl.pallas_call(functools.partial(backward_kernel, layers), out_shape=(jax...]
    all_gather x8, waiting for transfers between devices: 419 us -> 458 us  [local(): lax.all_gather(w[l], AXES, axis=0, tiled=True)]
    reduce_sum x12 -> x2, other arithmetic: 27.9 us -> 7.6 us  [the longest x1 6.96 us: local(): jnp.sum(valid * a * a)]
    convert_element_type x5 -> x7, other arithmetic: 25.2 us -> 6.02 us  [the longest x2 2.18 us: local(): pt = (ex / jnp.sum(ex, axis=2, keepdims=True)).astype(BF)]
    reshape x0 -> x6, local copies, waits for them, and re-layouts: none -> 13.9 us  [local(): q4, k4, v4 = (a.reshape(2, half, HEADS, hd) for a in (q, k, v))]
    concatenate x0 -> x3, other arithmetic: none -> 8.82 us  [turn(): jnp.concatenate([a, a], axis=0)]
  transfers between devices with their start and end apart: 8 -> 9, of which waited for: 8 -> 9; matrix products, arithmetic and copies ran while one was open for 18% -> 14% of each run, Pallas kernels for 0% -> 0%
where the time goes in v1:
time: 830 us; the launch traced here: 823 us
  waiting for transfers between devices  537 us (65%)
  matrix products  79.9 us (10%)
  Pallas kernels  74.8 us (9%)
  blocking collectives  39.3 us (5%)
  local copies, waits for them, and re-layouts  38.6 us (5%)
  other arithmetic  33.9 us (4%)
  between operations  18.6 us (2%)
    all_gather x8, waiting for transfers between devices, local(): lax.all_gather(w[l], AXES, axis=0, tiled=True)  458 us
    psum x1, waiting for transfers between devices, local(): lax.psum((grads[:, :10], jnp.stack(squares), count), AXES)  76.4 us
    pallas_call x1, Pallas kernels, backward(): pl.pallas_call(functools.partial(backward_kernel, layers), out_shape=(jax...  74.8 us
    dot_general x8, matrix products, nn(): lax.dot_general(a, b, (((1,), (0,)), ((), ())), preferred_element_type=F32)  69.7 us
    psum x1, blocking collectives, local(): lax.psum((grads[:, :10], jnp.stack(squares), count), AXES)  39.3 us
  transfers between devices with their start and end apart: 9, of which 9 were waited for; matrix products, arithmetic and copies ran while one was open for 14% of the time, Pallas kernels for 0%

profile of v1, /device:TPU:0, one launch (start us, length us, event | category | flops | bytes accessed | tf_op | source)
XLA Modules:
  0.0 822.6 jit_solution(7820017574727557140)
XLA Ops:
  24.6 58.9 %all-gather.17.cloned.1.call-done = bf16[1,1024,3072]{2,1,0:T(8,128)(2,1)} async-done(((bf16[1,32,3072]{2,1,0:T(8,128)(2,1)}), bf16[1,1024,3072]{2,1,0:T(8,128)(2,1)}) %all-gather.17.cloned.1.call-update) | async-done | bytes 6291472 | tf_op jit(solution)/shard_map/all_gather | solution.py:326
  83.5 6.5 fusion.108
  97.8 4.1 fusion.43
  110.7 30.7 %all-gather.19.cloned.1.call-done = bf16[1,1024,1024]{2,1,0:T(8,128)(2,1)} async-done(((bf16[1,32,1024]{2,1,0:T(8,128)(2,1)}), bf16[1,1024,1024]{2,1,0:T(8,128)(2,1)}) %all-gather.19.cloned.1.call-update) | async-done | bytes 2097168 | tf_op jit(solution)/shard_map/all_gather | solution.py:326
  141.4 5.2 fusion.117
  148.0 72.3 %all-gather.21.cloned.1.call-done = bf16[1,1024,4096]{2,1,0:T(8,128)(2,1)} async-done(((bf16[1,32,4096]{2,1,0:T(8,128)(2,1)}), bf16[1,1024,4096]{2,1,0:T(8,128)(2,1)}) %all-gather.21.cloned.1.call-update) | async-done | bytes 8388624 | tf_op jit(solution)/shard_map/all_gather | solution.py:326
  220.2 12.2 %fusion.6 = (bf16[512,4096]{1,0:T(8,128)(2,1)}, f32[512,4096]{1,0:T(8,128)}) fusion(f32[4096]{0:T(1024)S(1)} %bitcast.133, bf16[1,1024,4096]{2,1,0:T(8,128)(2,1)} %all-gather.21.cloned.1.call-done, f32[512,1024]{1,0:T(8,128)S(1)} %get-tuple-element.27, f32[1024]{0:T(1024)S(1)} %bitcast.143, f32[1024]{0:T(1024)S(1)} %bitcast.141, ...), kind=kOutput, calls=%fused_computation.8 | convolution fusion | flops 4318560256 | bytes 23097344 | tf_op jit(solution)/shard_map/dot_general | solution.py:18
  232.4 66.3 %all-gather.23.cloned.1.call-done = bf16[1,4096,1024]{2,1,0:T(8,128)(2,1)} async-done(((bf16[1,128,1024]{2,1,0:T(8,128)(2,1)}), bf16[1,4096,1024]{2,1,0:T(8,128)(2,1)}) %all-gather.23.cloned.1.call-update) | async-done | bytes 8388624 | tf_op jit(solution)/shard_map/all_gather | solution.py:326
  298.8 11.2 %fusion.116 = (f32[512]{0:T(512)S(1)}, f32[512,1024]{1,0:T(8,128)S(1)}, bf16[512,1024]{1,0:T(8,128)(2,1)}, f32[512,1024]{1,0:T(8,128)}) fusion(f32[1024]{0:T(1024)S(1)} %bitcast.117, f32[1024]{0:T(1024)S(1)} %bitcast.144, f32[1024]{0:T(1024)S(1)} %bitcast.142, f32[512]{0:T(512)S(1)} %add_rsqrt_fusion.3, f32[512,1024]{1,0:T(8,128)} %copy-done.16, ...), kind=kOutput, calls=%fused_computation.167 | convolution fusion | flops 4311744000 | bytes 24152064 | tf_op jit(solution)/shard_map/dot_general | solution.py:18
  310.3 59.1 %all-gather.25.cloned.1.call-done = bf16[1,1024,3072]{2,1,0:T(8,128)(2,1)} async-done(((bf16[1,32,3072]{2,1,0:T(8,128)(2,1)}), bf16[1,1024,3072]{2,1,0:T(8,128)(2,1)}) %all-gather.25.cloned.1.call-update) | async-done | bytes 6291472 | tf_op jit(solution)/shard_map/all_gather | solution.py:326
  369.4 5.9 fusion.70
  383.1 4.1 fusion.39
  394.5 32.6 %all-gather.27.cloned.1.call-done = bf16[1,1024,1024]{2,1,0:T(8,128)(2,1)} async-done(((bf16[1,32,1024]{2,1,0:T(8,128)(2,1)}), bf16[1,1024,1024]{2,1,0:T(8,128)(2,1)}) %all-gather.27.cloned.1.call-update) | async-done | bytes 2097168 | tf_op jit(solution)/shard_map/all_gather | solution.py:326
  427.1 4.4 fusion.115
  433.2 72.8 %all-gather.29.cloned.1.call-done = bf16[1,1024,4096]{2,1,0:T(8,128)(2,1)} async-done(((bf16[1,32,4096]{2,1,0:T(8,128)(2,1)}), bf16[1,1024,4096]{2,1,0:T(8,128)(2,1)}) %all-gather.29.cloned.1.call-update) | async-done | bytes 8388624 | tf_op jit(solution)/shard_map/all_gather | solution.py:326
  506.0 13.1 %fusion.11 = (bf16[512,4096]{1,0:T(8,128)(2,1)}, f32[512,4096]{1,0:T(8,128)}) fusion(f32[4096]{0:T(1024)S(1)} %bitcast.131, bf16[1,1024,4096]{2,1,0:T(8,128)(2,1)} %all-gather.29.cloned.1.call-done, f32[512,1024]{1,0:T(8,128)} %copy-done.15, f32[1024]{0:T(1024)S(1)} %bitcast.139, f32[1024]{0:T(1024)S(1)} %bitcast.137, f32[512]{0:T(512)S(1)} %add_rsqrt_fusion.1, ...), kind=kOutput, calls=%fused_computation.13 | convolution fusion | flops 4318560256 | bytes 23097344 | tf_op jit(solution)/shard_map/dot_general | solution.py:18
  519.1 65.6 %all-gather.31.cloned.1.call-done = bf16[1,4096,1024]{2,1,0:T(8,128)(2,1)} async-done(((bf16[1,128,1024]{2,1,0:T(8,128)(2,1)}), bf16[1,4096,1024]{2,1,0:T(8,128)(2,1)}) %all-gather.31.cloned.1.call-update) | async-done | bytes 8388624 | tf_op jit(solution)/shard_map/all_gather | solution.py:326
  584.6 11.2 %fusion.114 = (f32[512]{0:T(512)S(1)}, f32[512,1024]{1,0:T(8,128)S(1)}, bf16[512,1024]{1,0:T(8,128)(2,1)}, f32[512,1024]{1,0:T(8,128)}) fusion(f32[1024]{0:T(1024)S(1)} %bitcast.115, f32[1024]{0:T(1024)S(1)} %bitcast.140, f32[1024]{0:T(1024)S(1)} %bitcast.138, f32[512]{0:T(512)S(1)} %add_rsqrt_fusion.1, f32[512,1024]{1,0:T(8,128)} %copy-done.15, ...), kind=kOutput, calls=%fused_computation.165 | convolution fusion | flops 4311744000 | bytes 24152064 | tf_op jit(solution)/shard_map/dot_general | solution.py:18
  600.1 7.0 fusion.28
  607.1 4.0 maximum_bitcast_fusion
  612.9 74.8 %backward.1 = (f32[512,1024]{1,0:T(8,128)}, f32[2,16,1024]{2,1,0:T(8,128)}) custom-call(bf16[512,1024]{1,0:T(8,128)(2,1)} %fusion.76.refs_0_, f32[512,1]{1,0:T(8,128)} %fusion.93.refs_1_, f32[2,2,1024]{2,1,0:T(2,128)} %refs_2_.1, bf16[512,1024]{1,0:T(8,128)(2,1)} %copy-done.5, bf16[512,1024]{1,0:T(8,128)(2,1)} %copy-done.7, bf16[512,1024]{1,0:T(8,128)(2,1)} %copy-done.2, ...), custom_call_target="tpu_custom_call" | custom-call | tf_op jit(solution)/shard_map/backward/pallas_call | solution.py:257
  687.7 39.3 %all-reduce = (f32[2,3]{1,0:T(2,128)S(1)}, f32[]{:T(128)}) all-reduce(f32[2,3]{1,0:T(2,128)S(1)} %pad_maximum_fusion, f32[]{:T(128)S(6)} %convert_element_type.121), channel_id=1, replica_groups=mesh['dp'=8,'shard'=4] {'dp','shard'}, use_global_device_ids=true, to_apply=%region_19.20 | all-reduce | flops 7 | bytes 56 | tf_op jit(solution)/shard_map/psum | solution.py:353
  728.2 3.8 fusion.34
  734.6 76.4 %all-reduce.3.cloned.1.call-done = f32[2,10,1024]{2,1,0:T(8,128)} async-done(((f32[2,10,1024]{2,1,0:T(8,128)}), f32[2,10,1024]{2,1,0:T(8,128)}) %all-reduce.3.cloned.1.call-update) | async-done | bytes 81936 | tf_op jit(solution)/shard_map/psum | solution.py:353
  (138 shorter events, 62.6 us)
Async XLA Ops:
  7.2 5.7 copy-start.21
  7.2 76.3 %all-gather.17.cloned.1.call-start = ((), (), s32[]{:S(2)}) async-start(), calls=%async_computation.1 | async-start | bytes 6488064 | tf_op jit(solution)/shard_map/all_gather | solution.py:326
  9.1 7.4 copy-start.28
  9.1 12.1 %copy-start.24 = (f32[2,2,1024]{2,1,0:T(2,128)S(1)}, f32[2,2,1024]{2,1,0:T(2,128)}, u32[]{:S(2)}) copy-start(f32[2,2,1024]{2,1,0:T(2,128)} %param.20) | copy-start | bytes 49156
  9.1 12.2 %copy-start.26 = (f32[2,1024]{1,0:T(2,128)S(1)}, f32[2,1024]{1,0:T(2,128)}, u32[]{:S(2)}) copy-start(f32[2,1024]{1,0:T(2,128)} %param.21) | copy-start | bytes 24580
  9.1 12.2 %copy-start.22 = (f32[2,2,1024]{2,1,0:T(2,128)S(1)}, f32[2,2,1024]{2,1,0:T(2,128)}, u32[]{:S(2)}) copy-start(f32[2,2,1024]{2,1,0:T(2,128)} %refs_2_.1) | copy-start | bytes 49156
  9.1 12.3 %copy-start.25 = (f32[2,2,1024]{2,1,0:T(2,128)S(1)}, f32[2,2,1024]{2,1,0:T(2,128)}, u32[]{:S(2)}) copy-start(f32[2,2,1024]{2,1,0:T(2,128)} %param.22) | copy-start | bytes 49156
  9.1 132.2 %all-gather.19.cloned.1.call-start = ((), (), s32[]{:S(2)}) async-start(), calls=%async_computation.2 | async-start | bytes 2162688 | tf_op jit(solution)/shard_map/all_gather | solution.py:326
  10.7 10.7 %copy-start.23 = (f32[2,4096]{1,0:T(2,128)S(1)}, f32[2,4096]{1,0:T(2,128)}, u32[]{:S(2)}) copy-start(f32[2,4096]{1,0:T(2,128)} %param.23) | copy-start | bytes 98308
  10.7 10.7 %copy-start.27 = (f32[2,1024]{1,0:T(2,128)S(1)}, f32[2,1024]{1,0:T(2,128)}, u32[]{:S(2)}) copy-start(f32[2,1024]{1,0:T(2,128)} %param.24) | copy-start | bytes 24580
  10.7 11.4 %copy-start.20 = (bf16[512,1024]{1,0:T(8,128)(2,1)S(1)}, bf16[512,1024]{1,0:T(8,128)(2,1)}, u32[]{:S(2)}) copy-start(bf16[512,1024]{1,0:T(8,128)(2,1)} %param.25) | copy-start | bytes 3145732
  10.8 209.5 %all-gather.21.cloned.1.call-start = ((), (), s32[]{:S(2)}) async-start(), calls=%async_computation.3 | async-start | bytes 8650752 | tf_op jit(solution)/shard_map/all_gather | solution.py:326
  12.8 285.9 %all-gather.23.cloned.1.call-start = ((), (), s32[]{:S(2)}) async-start(), calls=%async_computation.4 | async-start | bytes 8650752 | tf_op jit(solution)/shard_map/all_gather | solution.py:326
  13.7 69.8 %copy-start.17 = (bf16[512,1024]{1,0:T(8,128)(2,1)S(1)}, bf16[512,1024]{1,0:T(8,128)(2,1)}, u32[]{:S(2)}) copy-start(bf16[512,1024]{1,0:T(8,128)(2,1)} %param.13) | copy-start | bytes 3145732
  13.8 355.6 %all-gather.25.cloned.1.call-start = ((), (), s32[]{:S(2)}) async-start(), calls=%async_computation.5 | async-start | bytes 6488064 | tf_op jit(solution)/shard_map/all_gather | solution.py:326
  14.4 412.7 %all-gather.27.cloned.1.call-start = ((), (), s32[]{:S(2)}) async-start(), calls=%async_computation.6 | async-start | bytes 2162688 | tf_op jit(solution)/shard_map/all_gather | solution.py:326
  14.9 491.1 %all-gather.29.cloned.1.call-start = ((), (), s32[]{:S(2)}) async-start(), calls=%async_computation.7 | async-start | bytes 8650752 | tf_op jit(solution)/shard_map/all_gather | solution.py:326
  15.7 569.0 %all-gather.31.cloned.1.call-start = ((), (), s32[]{:S(2)}) async-start(), calls=%async_computation.8 | async-start | bytes 8650752 | tf_op jit(solution)/shard_map/all_gather | solution.py:326
  16.4 794.6 %all-reduce.3.cloned.1.call-start = ((), (), s32[]{:S(2)}) async-start(), calls=%async_computation | async-start | bytes 262144 | tf_op jit(solution)/shard_map/psum | solution.py:353
  108.3 33.0 %copy-start.18 = (bf16[512,1024]{1,0:T(8,128)(2,1)S(1)}, bf16[512,1024]{1,0:T(8,128)(2,1)}, u32[]{:S(2)}) copy-start(bf16[512,1024]{1,0:T(8,128)(2,1)} %param.13) | copy-start | bytes 3145732
  146.5 85.9 %copy-start.16 = (f32[512,1024]{1,0:T(8,128)}, f32[512,1024]{1,0:T(8,128)S(1)}, u32[]{:S(2)}) copy-start(f32[512,1024]{1,0:T(8,128)S(1)} %get-tuple-element.27) | copy-start | bytes 6291460
  309.9 59.5 %copy-start.8 = (f32[512,1024]{1,0:T(8,128)}, f32[512,1024]{1,0:T(8,128)S(1)}, u32[]{:S(2)}) copy-start(f32[512,1024]{1,0:T(8,128)S(1)} %get-tuple-element.25) | copy-start | bytes 6291460
  393.2 33.9 %copy-start.9 = (f32[512,1024]{1,0:T(8,128)S(1)}, f32[512,1024]{1,0:T(8,128)}, u32[]{:S(2)}) copy-start(f32[512,1024]{1,0:T(8,128)} %copy-done.8) | copy-start | bytes 6291460
  600.1 10.9 %copy-start.13 = (f32[512,1024]{1,0:T(8,128)S(1)}, f32[512,1024]{1,0:T(8,128)}, u32[]{:S(2)}) copy-start(f32[512,1024]{1,0:T(8,128)} %copy-done.12) | copy-start | bytes 6291460
  (14 other events, 42.3 us)
Sparse Core Ops, SparseCore 0:
  11.4 72.0 all-gather.16
  86.4 54.8 all-gather.18
  144.3 75.9 all-gather.20
  223.0 75.6 all-gather.22
  301.5 67.8 all-gather.24
  372.2 54.8 all-gather.26
  430.0 75.9 all-gather.28
  508.9 75.6 all-gather.30
  687.8 123.1 all-reduce.2
